TPU v7x, 32 devices: a whole 2x2x4 slice. The times are simulated.
32 devices in a mesh: orb: 4 (over z), tile: 8 (over y, x, core).
Axes of the slice: x: 2, y: 2, z: 4, core: 2. Of those that a mesh axis runs over, the one named last changes fastest.
Arguments:
- basis_values: bfloat16 [2048, 65536], P('tile'), may hold values from -6 to 6
- coefficients: bfloat16 [65536, 128], P('tile', 'orb'), may hold values from -0.03125 to 0.03125
- occupations: float32 [128], P('orb'), may hold values from 0.5 to 2
- owners: int32 [2048, 1], P('tile'), may hold values from 0 to 7; in each aligned block of 256 rows (0 to 255, 256 to 511, ...) at most 64 rows name the same one
- offsets: int32 [2048], P('tile'), may hold values from 0 to 8191
Outputs:
- density: float32 [64, 64, 128], P('tile', 'orb')
- gradient: float32 [3, 64, 64, 128], P(None, 'tile', 'orb')
Inputs may be any that keep to these rules, and one draw needn't show every extreme that they name: `owners`: at most 64 entries of one tile's list name the same owner, and some tile's list reaches 64.
All inputs are finite; a program needn't handle non-finite values.
Results may differ from a plain program's by a relative error of at most 0.0003.
Values may be sent and summed in bfloat16 or wider, within the bound.
A program may use at most 320 MiB of HBM per device.

v0:
```python
import jax
import jax.numpy as jnp
from jax import lax
from jax.sharding import PartitionSpec as P

CY = 64
CZ = 128


def with_halo(cells, sides, width):
    for axis, dim in sides:
        count = lax.axis_size(axis)
        ends = count - 1
        head = lax.slice_in_dim(cells, 0, width, axis=dim)
        tail = lax.slice_in_dim(cells, cells.shape[dim] - width, cells.shape[dim], axis=dim)
        cells = jnp.concatenate(
            [
                lax.ppermute(tail, axis, [(i, (i + 1) % count) for i in range(ends)]),
                cells,
                lax.ppermute(head, axis, [((i + 1) % count, i) for i in range(ends)]),
            ],
            axis=dim,
        )
    return cells


def central(padded):
    along_x = 0.5 * (padded[2:, 1:-1, 1:-1] - padded[:-2, 1:-1, 1:-1])
    along_y = 0.5 * (padded[1:-1, 2:, 1:-1] - padded[1:-1, :-2, 1:-1])
    along_z = 0.5 * (padded[1:-1, 1:-1, 2:] - padded[1:-1, 1:-1, :-2])
    return jnp.stack([along_x, along_y, along_z])


def body(basis_values, coefficients, occupations, owners, offsets):
    listed_count = owners.shape[0]
    rows_held = coefficients.shape[0]
    local_orbitals = coefficients.shape[1]
    owner_ids = owners[:, 0]
    global_rows = owner_ids * rows_held + offsets
    empty = jnp.zeros((listed_count, local_orbitals), jnp.bfloat16)
    shard_rows = lax.all_gather(coefficients, "tile", axis=0, tiled=True)
    inside = (global_rows >= 0) & (global_rows < shard_rows.shape[0])
    safe_rows = jnp.clip(global_rows, 0, shard_rows.shape[0] - 1)
    taken = jnp.take(shard_rows, safe_rows, axis=0)
    listed = jnp.where(inside[:, None], taken, empty)
    depth_cells = basis_values.shape[1] // (CY * CZ)
    share_width = CY // lax.axis_size("orb")
    orbitals = jnp.einsum("bo,bc->oc", listed, basis_values, preferred_element_type=jnp.float32)
    partial_value = jnp.sum(occupations[:, None] * orbitals * orbitals, axis=0).reshape(
        depth_cells, CY, CZ
    )
    density_full = lax.psum(partial_value, "orb")
    padded = with_halo(density_full, (("tile", 0),), 1)
    padded = jnp.pad(padded, ((0, 0), (1, 1), (1, 1)))
    first_col = lax.axis_index("orb") * share_width
    density = lax.dynamic_slice_in_dim(density_full, first_col, share_width, 1)
    gradient = lax.dynamic_slice_in_dim(central(padded), first_col, share_width, 2)
    return (density, gradient)


def solution(mesh):
    placed = (P("tile", None), P("tile", "orb"), P("orb"), P("tile", None), P("tile"))
    return jax.shard_map(
        body,
        mesh=mesh,
        in_specs=placed,
        out_specs=(P("tile", "orb", None), P(None, "tile", "orb", None)),
        check_vma=False,
    )
```

profile of v0, /device:TPU:4, one launch (start us, length us, event | category | flops | bytes accessed | tf_op | source)
XLA Modules:
  0.0 181.8 jit_solution(3366293693858491619)
XLA Ops:
  7.2 0.0 all-gather.2.cloned.1.call-start
  7.2 2.7 %copy.7 = bf16[8192,32]{1,0:T(8,128)(2,1)} copy(bf16[8192,32]{0,1:T(8,128)(2,1)} %param.6) | data formatting | bytes 1048576 | tf_op args[1]
  9.9 0.0 all-gather.2.cloned.1.call-update
  9.9 0.0 all-reduce.3.cloned.1.call-start
  10.0 0.7 broadcast_multiply_fusion
  10.6 0.7 compare_and_fusion
  11.3 88.9 %all-gather.2.cloned.1.call-done = bf16[65536,32]{1,0:T(8,128)(2,1)} async-done(((bf16[8192,32]{1,0:T(8,128)(2,1)}), bf16[65536,32]{1,0:T(8,128)(2,1)}) %all-gather.2.cloned.1.call-update) | async-done | bytes 4194320 | tf_op jit(solution)/shard_map/all_gather | solution.py:41
  100.3 8.7 %gather_fusion = bf16[256,32]{1,0:T(8,128)(2,1)S(1)} fusion(bf16[65536,32]{1,0:T(8,128)(2,1)} %all-gather.2.cloned.1.call-done, s32[1024]{0:T(1024)S(1)} %pad_clamp_fusion), kind=kCustom, calls=%fused_computation | custom fusion | bytes 33792 | tf_op jit(solution)/shard_map/jit(_take)/gather | solution.py:44
  108.9 17.4 %fusion = f32[65536]{0:T(1024)} fusion(f32[32]{0:T(128)} %param.7, bf16[256,65536]{1,0:T(8,128)(2,1)} %param.5, bf16[256,32]{1,0:T(8,128)(2,1)S(1)} %gather_fusion, pred[256]{0:T(512)(128)(4,1)S(1)} %get-tuple-element.2, pred[256]{0:T(512)(128)(4,1)S(1)} %get-tuple-element.8), kind=kOutput, calls=%fused_computation.2 | convolution fusion | flops 1079984128 | bytes 33833600 | tf_op jit(solution)/shard_map/bo,bc->oc/dot_general | solution.py:48
  126.3 0.0 all-reduce.3.cloned.1.call-update
  126.4 36.5 %all-reduce.3.cloned.1.call-done = f32[8,64,128]{2,1,0:T(8,128)} async-done(((f32[8,64,128]{2,1,0:T(8,128)}), f32[8,64,128]{2,1,0:T(8,128)}) %all-reduce.3.cloned.1.call-update) | async-done | bytes 262160 | tf_op jit(solution)/shard_map/psum | solution.py:52
  162.8 0.8 fusion.24
  163.6 1.9 %collective-permute-start = (f32[1,64,128]{2,1,0:T(8,128)S(1)}, f32[1,64,128]{2,1,0:T(8,128)S(1)}, u32[]{:S(2)}, u32[]{:S(2)}) collective-permute-start(f32[1,64,128]{2,1,0:T(8,128)S(1)} %get-tuple-element.6), channel_id=1, source_target_pairs={{1,0},{2,1},{3,2},{4,3},{5,4},{6,5},{7,6},{9,8},{10,9},{11,10},{12... | collective-permute-start | bytes 98312 | tf_op jit(solution)/shard_map/ppermute | solution.py:20
  165.5 2.4 %collective-permute-start.1 = (f32[1,64,128]{2,1,0:T(8,128)S(1)}, f32[1,64,128]{2,1,0:T(8,128)S(1)}, u32[]{:S(2)}, u32[]{:S(2)}) collective-permute-start(f32[1,64,128]{2,1,0:T(8,128)S(1)} %get-tuple-element.7), channel_id=1, source_target_pairs={{0,1},{1,2},{2,3},{3,4},{4,5},{5,6},{6,7},{8,9},{9,10},{10,11},{11... | collective-permute-start | bytes 98312 | tf_op jit(solution)/shard_map/ppermute | solution.py:18
  167.9 1.5 constant_dynamic-slice_fusion
  169.4 0.0 collective-permute-done
  169.4 2.2 %collective-permute-done.1 = f32[1,64,128]{2,1,0:T(8,128)S(1)} collective-permute-done((f32[1,64,128]{2,1,0:T(8,128)S(1)}, f32[1,64,128]{2,1,0:T(8,128)S(1)}, u32[]{:S(2)}, u32[]{:S(2)}) %collective-permute-start.1) | collective-permute-done | bytes 32800 | tf_op jit(solution)/shard_map/ppermute | solution.py:18
  171.7 1.2 select_maximum_fusion
  172.9 1.3 fusion.5
  174.2 0.7 fusion.12
  (1 shorter events, 0.0 us)
Async XLA Ops:
  7.2 93.1 %all-gather.2.cloned.1.call-start = ((), (), s32[]{:S(2)}) async-start(), calls=%async_computation | async-start | bytes 18874368 | tf_op jit(solution)/shard_map/all_gather | solution.py:41
  9.9 152.9 %all-reduce.3.cloned.1.call-start = ((), (), s32[]{:S(2)}) async-start(), calls=%async_computation.1 | async-start | bytes 524288 | tf_op jit(solution)/shard_map/psum | solution.py:52
  163.6 5.8 %collective-permute-start = (f32[1,64,128]{2,1,0:T(8,128)S(1)}, f32[1,64,128]{2,1,0:T(8,128)S(1)}, u32[]{:S(2)}, u32[]{:S(2)}) collective-permute-start(f32[1,64,128]{2,1,0:T(8,128)S(1)} %get-tuple-element.6), channel_id=1, source_target_pairs={{1,0},{2,1},{3,2},{4,3},{5,4},{6,5},{7,6},{9,8},{10,9},{11,10},{12... | collective-permute-start | bytes 98312 | tf_op jit(solution)/shard_map/ppermute | solution.py:20
  165.5 6.1 %collective-permute-start.1 = (f32[1,64,128]{2,1,0:T(8,128)S(1)}, f32[1,64,128]{2,1,0:T(8,128)S(1)}, u32[]{:S(2)}, u32[]{:S(2)}) collective-permute-start(f32[1,64,128]{2,1,0:T(8,128)S(1)} %get-tuple-element.7), channel_id=1, source_target_pairs={{0,1},{1,2},{2,3},{3,4},{4,5},{5,6},{6,7},{8,9},{9,10},{10,11},{11... | collective-permute-start | bytes 98312 | tf_op jit(solution)/shard_map/ppermute | solution.py:18
Sparse Core Ops, SparseCore 0:
  10.0 90.1 all-gather.1
  126.5 36.3 all-reduce.2
where the time goes:
time: 182 us
  waiting for transfers between devices  128 us (70%)
  matrix products  17.4 us (10%)
  between operations  14.1 us (8%)
  local copies, waits for them, and re-layouts  13.6 us (7%)
  other arithmetic  4.62 us (3%)
  starting transfers between devices  4.39 us (2%)
    all_gather x1, waiting for transfers between devices, body(): shard_rows = lax.all_gather(coefficients, 'tile', axis=0, tiled=True)  88.9 us
    psum x1, waiting for transfers between devices, body(): density_full = lax.psum(partial_value, 'orb')  36.5 us
    dot_general x1, matrix products, body(): jnp.einsum('bo,bc->oc', listed, basis_values, preferred_element_type=jnp....  17.4 us
    gather x1, local copies, waits for them, and re-layouts, body(): taken = jnp.take(shard_rows, safe_rows, axis=0)  8.65 us
  transfers between devices with their start and end apart: 4, of which 3 were waited for; matrix products, arithmetic and copies ran while one was open for 2% of the time, Pallas kernels for 0%

commit v1 on v0

--- a/solution.py
+++ b/solution.py
@@ -5,6 +5,16 @@
 
 CY = 64
 CZ = 128
+
+
+def ring_gather(x, axis, dim):
+    ways, here, lap = (lax.axis_size(axis), lax.axis_index(axis), x.shape[dim])
+    lengths = [n * ways if d == dim else n for d, n in enumerate(x.shape)]
+    full = lax.dynamic_update_slice_in_dim(jnp.zeros(lengths, x.dtype), x, here * lap, axis=dim)
+    for far in range(1, ways):
+        x = lax.ppermute(x, axis, [(d, (d + 1) % ways) for d in range(ways)])
+        full = lax.dynamic_update_slice_in_dim(full, x, (here - far) % ways * lap, axis=dim)
+    return full
 
 
 def with_halo(cells, sides, width):
@@ -38,7 +48,7 @@
     owner_ids = owners[:, 0]
     global_rows = owner_ids * rows_held + offsets
     empty = jnp.zeros((listed_count, local_orbitals), jnp.bfloat16)
-    shard_rows = lax.all_gather(coefficients, "tile", axis=0, tiled=True)
+    shard_rows = ring_gather(coefficients, "tile", 0)
     inside = (global_rows >= 0) & (global_rows < shard_rows.shape[0])
     safe_rows = jnp.clip(global_rows, 0, shard_rows.shape[0] - 1)
     taken = jnp.take(shard_rows, safe_rows, axis=0)

time: 182 us -> 165 us (0.907)
  waiting for transfers between devices: 128 us -> 85 us
  local copies, waits for them, and re-layouts: 13.6 us -> 37.8 us
  starting transfers between devices: 4.39 us -> 6.47 us
    all_gather x1 -> x0, waiting for transfers between devices: 88.9 us -> none  [body(): shard_rows = lax.all_gather(coefficients, 'tile', axis=0, tiled=True)]
    ppermute x0 -> x7, waiting for transfers between devices: none -> 46.7 us  [ring_gather(): x = lax.ppermute(x, axis, [(d, (d + 1) % ways) for d in range(ways)])]
    dynamic_update_slice x0 -> x8, local copies, waits for them, and re-layouts: none -> 11.7 us  [the longest x7 10.2 us: ring_gather(): lax.dynamic_update_slice_in_dim(full, x, (here - far) % ways * lap, axis=...]
    ppermute x0 -> x7, local copies, waits for them, and re-layouts: none -> 7.21 us  [ring_gather(): x = lax.ppermute(x, axis, [(d, (d + 1) % ways) for d in range(ways)])]
    broadcast_in_dim x0 -> x1, local copies, waits for them, and re-layouts: none -> 6.02 us  [ring_gather(): jnp.zeros(lengths, x.dtype)]
    ppermute x0 -> x7, starting transfers between devices: none -> 2.11 us  [ring_gather(): x = lax.ppermute(x, axis, [(d, (d + 1) % ways) for d in range(ways)])]
  transfers between devices with their start and end apart: 4 -> 10, of which waited for: 3 -> 8; matrix products, arithmetic and copies ran while one was open for 2% -> 12% of each run, Pallas kernels for 0% -> 0%
where the time goes in v1:
time: 165 us; the launch traced here: 164 us
  waiting for transfers between devices  85 us (52%)
  local copies, waits for them, and re-layouts  37.8 us (23%)
  matrix products  17.4 us (11%)
  between operations  14.4 us (9%)
  starting transfers between devices  6.47 us (4%)
  other arithmetic  3.26 us (2%)
    ppermute x7, waiting for transfers between devices, ring_gather(): x = lax.ppermute(x, axis, [(d, (d + 1) % ways) for d in range(ways)])  46.7 us
    psum x1, waiting for transfers between devices, body(): density_full = lax.psum(partial_value, 'orb')  36 us
    dot_general x1, matrix products, body(): jnp.einsum('bo,bc->oc', listed, basis_values, preferred_element_type=jnp....  17.4 us
    dynamic_update_slice x7, local copies, waits for them, and re-layouts, ring_gather(): lax.dynamic_update_slice_in_dim(full, x, (here - far) % ways * lap, axis=...  10.2 us
    gather x1, local copies, waits for them, and re-layouts, body(): taken = jnp.take(shard_rows, safe_rows, axis=0)  8.65 us
    ppermute x7, local copies, waits for them, and re-layouts, ring_gather(): x = lax.ppermute(x, axis, [(d, (d + 1) % ways) for d in range(ways)])  7.21 us
    broadcast_in_dim x1, local copies, waits for them, and re-layouts, ring_gather(): jnp.zeros(lengths, x.dtype)  6.02 us
  transfers between devices with their start and end apart: 10, of which 8 were waited for; matrix products, arithmetic and copies ran while one was open for 12% of the time, Pallas kernels for 0%

profile of v1, /device:TPU:4, one launch (start us, length us, event | category | flops | bytes accessed | tf_op | source)
XLA Modules:
  0.0 164.3 jit_solution(10770106793513225132)
XLA Ops:
  7.3 1.9 %copy.9 = bf16[8192,32]{1,0:T(8,128)(2,1)S(1)} copy(bf16[8192,32]{0,1:T(8,128)(2,1)} %param.6) | data formatting | bytes 1048576 | tf_op args[1]
  9.4 6.0 %broadcast_in_dim.30 = bf16[65536,32]{1,0:T(8,128)(2,1)} broadcast(bf16[]{:T(256)} %constant.84.clone.1), dimensions={} | broadcast | bytes 4194306 | tf_op jit(solution)/shard_map/broadcast_in_dim | solution.py:13
  15.4 1.5 constant_dynamic-update-slice_fusion.7
  17.0 1.0 copy.10
  18.0 1.6 collective-permute-start.1
  19.6 1.5 constant_dynamic-update-slice_fusion.6
  21.1 6.5 %collective-permute-done.1 = bf16[8192,32]{0,1:T(8,128)(2,1)S(1)} collective-permute-done((bf16[8192,32]{0,1:T(8,128)(2,1)S(1)}, bf16[8192,32]{0,1:T(8,128)(2,1)S(1)}, u32[]{:S(2)}, u32[]{:S(2)}) %collective-permute-start.1) | collective-permute-done | bytes 524320 | tf_op jit(solution)/shard_map/ppermute | solution.py:15
  27.6 1.0 copy.11
  28.7 1.5 constant_dynamic-update-slice_fusion.5
  30.2 8.0 %collective-permute-done.2 = bf16[8192,32]{0,1:T(8,128)(2,1)S(1)} collective-permute-done((bf16[8192,32]{0,1:T(8,128)(2,1)S(1)}, bf16[8192,32]{0,1:T(8,128)(2,1)S(1)}, u32[]{:S(2)}, u32[]{:S(2)}) %collective-permute-start.2) | collective-permute-done | bytes 524320 | tf_op jit(solution)/shard_map/ppermute | solution.py:15
  38.2 1.0 copy.12
  39.3 1.5 constant_dynamic-update-slice_fusion.4
  40.7 8.0 %collective-permute-done.3 = bf16[8192,32]{0,1:T(8,128)(2,1)S(1)} collective-permute-done((bf16[8192,32]{0,1:T(8,128)(2,1)S(1)}, bf16[8192,32]{0,1:T(8,128)(2,1)S(1)}, u32[]{:S(2)}, u32[]{:S(2)}) %collective-permute-start.3) | collective-permute-done | bytes 524320 | tf_op jit(solution)/shard_map/ppermute | solution.py:15
  48.8 1.0 copy.13
  49.9 1.5 constant_dynamic-update-slice_fusion.3
  51.4 8.0 %collective-permute-done.4 = bf16[8192,32]{0,1:T(8,128)(2,1)S(1)} collective-permute-done((bf16[8192,32]{0,1:T(8,128)(2,1)S(1)}, bf16[8192,32]{0,1:T(8,128)(2,1)S(1)}, u32[]{:S(2)}, u32[]{:S(2)}) %collective-permute-start.4) | collective-permute-done | bytes 524320 | tf_op jit(solution)/shard_map/ppermute | solution.py:15
  60.5 1.4 constant_dynamic-update-slice_fusion.2
  61.9 8.1 %collective-permute-done.5 = bf16[8192,32]{0,1:T(8,128)(2,1)S(1)} collective-permute-done((bf16[8192,32]{0,1:T(8,128)(2,1)S(1)}, bf16[8192,32]{0,1:T(8,128)(2,1)S(1)}, u32[]{:S(2)}, u32[]{:S(2)}) %collective-permute-start.5) | collective-permute-done | bytes 524320 | tf_op jit(solution)/shard_map/ppermute | solution.py:15
  70.0 1.0 copy.15
  71.3 1.5 constant_dynamic-update-slice_fusion.1
  72.7 8.0 %collective-permute-done.6 = bf16[8192,32]{0,1:T(8,128)(2,1)S(1)} collective-permute-done((bf16[8192,32]{0,1:T(8,128)(2,1)S(1)}, bf16[8192,32]{0,1:T(8,128)(2,1)S(1)}, u32[]{:S(2)}, u32[]{:S(2)}) %collective-permute-start.6) | collective-permute-done | bytes 524320 | tf_op jit(solution)/shard_map/ppermute | solution.py:15
  80.8 1.0 copy.16
  81.8 1.5 constant_dynamic-update-slice_fusion
  83.2 8.7 %gather_fusion = bf16[256,32]{1,0:T(8,128)(2,1)S(1)} fusion(bf16[65536,32]{1,0:T(8,128)(2,1)} %constant_dynamic-update-slice_fusion, s32[1024]{0:T(1024)S(1)} %pad_clamp_fusion), kind=kCustom, calls=%fused_computation | custom fusion | bytes 33792 | tf_op jit(solution)/shard_map/jit(_take)/gather | solution.py:54
  91.9 17.4 %fusion = f32[65536]{0:T(1024)} fusion(f32[32]{0:T(128)S(1)} %copy-done.2, bf16[256,65536]{1,0:T(8,128)(2,1)} %param.5, bf16[256,32]{1,0:T(8,128)(2,1)S(1)} %gather_fusion, pred[256]{0:T(512)(128)(4,1)S(1)} %get-tuple-element.2, pred[256]{0:T(512)(128)(4,1)S(1)} %get-tuple-element.8), kind=kOutput, calls=%fused_computation.2 | convolution fusion | flops 1079984128 | bytes 33833600 | tf_op jit(solution)/shard_map/bo,bc->oc/dot_general | solution.py:58
  109.4 36.0 %all-reduce.3.cloned.1.call-done = f32[8,64,128]{2,1,0:T(8,128)} async-done(((f32[8,64,128]{2,1,0:T(8,128)}), f32[8,64,128]{2,1,0:T(8,128)}) %all-reduce.3.cloned.1.call-update) | async-done | bytes 262160 | tf_op jit(solution)/shard_map/psum | solution.py:62
  146.2 1.9 %collective-permute-start.7 = (f32[1,64,128]{2,1,0:T(8,128)S(1)}, f32[1,64,128]{2,1,0:T(8,128)S(1)}, u32[]{:S(2)}, u32[]{:S(2)}) collective-permute-start(f32[1,64,128]{2,1,0:T(8,128)S(1)} %get-tuple-element.6), channel_id=1, source_target_pairs={{1,0},{2,1},{3,2},{4,3},{5,4},{6,5},{7,6},{9,8},{10,9},{11,10},{12... | collective-permute-start | bytes 98312 | tf_op jit(solution)/shard_map/ppermute | solution.py:30
  148.1 2.4 %collective-permute-start.8 = (f32[1,64,128]{2,1,0:T(8,128)S(1)}, f32[1,64,128]{2,1,0:T(8,128)S(1)}, u32[]{:S(2)}, u32[]{:S(2)}) collective-permute-start(f32[1,64,128]{2,1,0:T(8,128)S(1)} %get-tuple-element.7), channel_id=1, source_target_pairs={{0,1},{1,2},{2,3},{3,4},{4,5},{5,6},{6,7},{8,9},{9,10},{10,11},{11... | collective-permute-start | bytes 98312 | tf_op jit(solution)/shard_map/ppermute | solution.py:28
  150.5 1.5 constant_dynamic-slice_fusion
  152.0 2.2 %collective-permute-done.8 = f32[1,64,128]{2,1,0:T(8,128)S(1)} collective-permute-done((f32[1,64,128]{2,1,0:T(8,128)S(1)}, f32[1,64,128]{2,1,0:T(8,128)S(1)}, u32[]{:S(2)}, u32[]{:S(2)}) %collective-permute-start.8) | collective-permute-done | bytes 32800 | tf_op jit(solution)/shard_map/ppermute | solution.py:28
  154.2 1.2 select_maximum_fusion
  155.4 1.3 fusion.5
  (22 shorter events, 3.2 us)
Async XLA Ops:
  7.2 9.8 %copy-start = (s32[256,1]{0,1:T(1,128)S(1)}, s32[256,1]{0,1:T(1,128)}, u32[]{:S(2)}) copy-start(s32[256,1]{0,1:T(1,128)} %param.8) | copy-start | bytes 3076
  7.2 9.8 %copy-start.1 = (s32[256]{0:T(256)S(1)}, s32[256]{0:T(256)}, u32[]{:S(2)}) copy-start(s32[256]{0:T(256)} %param.9) | copy-start | bytes 3076
  7.2 138.2 %all-reduce.3.cloned.1.call-start = ((), (), s32[]{:S(2)}) async-start(), calls=%async_computation | async-start | bytes 524288 | tf_op jit(solution)/shard_map/psum | solution.py:62
  7.2 9.8 %collective-permute-start = (bf16[8192,32]{0,1:T(8,128)(2,1)}, bf16[8192,32]{0,1:T(8,128)(2,1)S(1)}, u32[]{:S(2)}, u32[]{:S(2)}) collective-permute-start(bf16[8192,32]{0,1:T(8,128)(2,1)} %param.6), channel_id=1, source_target_pairs={{0,1},{1,2},{2,3},{3,4},{4,5},{5,6},{6,7},{7,0},{8,9},{9,10},{10,1... | collective-permute-start | bytes 1572872 | tf_op jit(solution)/shard_map/ppermute | solution.py:15
  18.0 9.6 %collective-permute-start.1 = (bf16[8192,32]{0,1:T(8,128)(2,1)S(1)}, bf16[8192,32]{0,1:T(8,128)(2,1)S(1)}, u32[]{:S(2)}, u32[]{:S(2)}) collective-permute-start(bf16[8192,32]{0,1:T(8,128)(2,1)S(1)} %collective-permute-done), channel_id=1, source_target_pairs={{0,1},{1,2},{2,3},{3,4},{4,5},{5,6},{6,7},{7,0},{8,9},{9,10},{10,1... | collective-permute-start | bytes 1572872 | tf_op jit(solution)/shard_map/ppermute | solution.py:15
  28.6 9.6 %collective-permute-start.2 = (bf16[8192,32]{0,1:T(8,128)(2,1)S(1)}, bf16[8192,32]{0,1:T(8,128)(2,1)S(1)}, u32[]{:S(2)}, u32[]{:S(2)}) collective-permute-start(bf16[8192,32]{0,1:T(8,128)(2,1)S(1)} %collective-permute-done.1), channel_id=1, source_target_pairs={{0,1},{1,2},{2,3},{3,4},{4,5},{5,6},{6,7},{7,0},{8,9},{9,10},{10,1... | collective-permute-start | bytes 1572872 | tf_op jit(solution)/shard_map/ppermute | solution.py:15
  30.2 61.7 %copy-start.2 = (f32[32]{0:T(128)S(1)}, f32[32]{0:T(128)}, u32[]{:S(2)}) copy-start(f32[32]{0:T(128)} %param.7) | copy-start | bytes 388
  39.2 9.6 %collective-permute-start.3 = (bf16[8192,32]{0,1:T(8,128)(2,1)S(1)}, bf16[8192,32]{0,1:T(8,128)(2,1)S(1)}, u32[]{:S(2)}, u32[]{:S(2)}) collective-permute-start(bf16[8192,32]{0,1:T(8,128)(2,1)S(1)} %collective-permute-done.2), channel_id=1, source_target_pairs={{0,1},{1,2},{2,3},{3,4},{4,5},{5,6},{6,7},{7,0},{8,9},{9,10},{10,1... | collective-permute-start | bytes 1572872 | tf_op jit(solution)/shard_map/ppermute | solution.py:15
  49.8 9.6 %collective-permute-start.4 = (bf16[8192,32]{0,1:T(8,128)(2,1)S(1)}, bf16[8192,32]{0,1:T(8,128)(2,1)S(1)}, u32[]{:S(2)}, u32[]{:S(2)}) collective-permute-start(bf16[8192,32]{0,1:T(8,128)(2,1)S(1)} %collective-permute-done.3), channel_id=1, source_target_pairs={{0,1},{1,2},{2,3},{3,4},{4,5},{5,6},{6,7},{7,0},{8,9},{9,10},{10,1... | collective-permute-start | bytes 1572872 | tf_op jit(solution)/shard_map/ppermute | solution.py:15
  60.4 9.6 %collective-permute-start.5 = (bf16[8192,32]{0,1:T(8,128)(2,1)S(1)}, bf16[8192,32]{0,1:T(8,128)(2,1)S(1)}, u32[]{:S(2)}, u32[]{:S(2)}) collective-permute-start(bf16[8192,32]{0,1:T(8,128)(2,1)S(1)} %collective-permute-done.4), channel_id=1, source_target_pairs={{0,1},{1,2},{2,3},{3,4},{4,5},{5,6},{6,7},{7,0},{8,9},{9,10},{10,1... | collective-permute-start | bytes 1572872 | tf_op jit(solution)/shard_map/ppermute | solution.py:15
  71.0 9.7 %collective-permute-start.6 = (bf16[8192,32]{0,1:T(8,128)(2,1)S(1)}, bf16[8192,32]{0,1:T(8,128)(2,1)S(1)}, u32[]{:S(2)}, u32[]{:S(2)}) collective-permute-start(bf16[8192,32]{0,1:T(8,128)(2,1)S(1)} %collective-permute-done.5), channel_id=1, source_target_pairs={{0,1},{1,2},{2,3},{3,4},{4,5},{5,6},{6,7},{7,0},{8,9},{9,10},{10,1... | collective-permute-start | bytes 1572872 | tf_op jit(solution)/shard_map/ppermute | solution.py:15
  146.2 5.8 %collective-permute-start.7 = (f32[1,64,128]{2,1,0:T(8,128)S(1)}, f32[1,64,128]{2,1,0:T(8,128)S(1)}, u32[]{:S(2)}, u32[]{:S(2)}) collective-permute-start(f32[1,64,128]{2,1,0:T(8,128)S(1)} %get-tuple-element.6), channel_id=1, source_target_pairs={{1,0},{2,1},{3,2},{4,3},{5,4},{6,5},{7,6},{9,8},{10,9},{11,10},{12... | collective-permute-start | bytes 98312 | tf_op jit(solution)/shard_map/ppermute | solution.py:30
  148.1 6.1 %collective-permute-start.8 = (f32[1,64,128]{2,1,0:T(8,128)S(1)}, f32[1,64,128]{2,1,0:T(8,128)S(1)}, u32[]{:S(2)}, u32[]{:S(2)}) collective-permute-start(f32[1,64,128]{2,1,0:T(8,128)S(1)} %get-tuple-element.7), channel_id=1, source_target_pairs={{0,1},{1,2},{2,3},{3,4},{4,5},{5,6},{6,7},{8,9},{9,10},{10,11},{11... | collective-permute-start | bytes 98312 | tf_op jit(solution)/shard_map/ppermute | solution.py:28
Sparse Core Ops, SparseCore 0:
  109.5 35.8 all-reduce.2
